TPU v7x, 128 devices: a whole 4x4x4 slice. The times are simulated.
128 devices in a mesh: dev: 128 (over y, x, z, core).
Axes of the slice: x: 4, y: 4, z: 4, core: 2. Of those that a mesh axis runs over, the one named last changes fastest.
Arguments:
- params: float32 [59, 262144], P(None, 'dev'), as said below
- blocks: int32 [512, 32], P('dev'), may hold values from 0 to 2047, as said below
- counts: int32 [512], P('dev'), may hold values from 4 to 32, as said below
- pixel_grad: float32 [3, 524288], P(None, 'dev'), may hold values from -192 to 192
Outputs:
- param_grad: float32 [59, 262144], P(None, 'dev')
Inputs may be any that keep to these rules, and one draw needn't show every extreme that they name: Block b is owned by device b // 16. Within the tiles of one device no block appears twice, and for every owner exactly 1 of that device's 4 * 32 slots, used or not, name its blocks. `counts`: in every draw all tiles of some one device have 32 used slots. `params`: row 2, the depth, lies from 3 to 6; row 6 from 1 to 2; row 10 below -2.
All inputs are finite; a program needn't handle non-finite values.
Results may differ from a plain program's by a relative error of at most 0.0003.
Values sent between devices are 32-bit elements; how exact they have to be, the bound alone decides.
A program may use at most 128 MiB of HBM per device.

v0:
```python
import jax
import jax.numpy as jnp
from jax import lax
from jax.sharding import PartitionSpec as P

BLOCK = 128
TILE_SIDE = 32
TILES_X = 32
sh_zero = 0.28209479177387814
sh_one = 0.4886025119029199
sh_two = [
    1.0925484305920792,
    -1.0925484305920792,
    0.31539156525252005,
    -1.0925484305920792,
    0.5462742152960396,
]
sh_three = [
    -0.5900435899266435,
    2.890611442640554,
    -0.4570457994644658,
    0.3731763325901154,
    -0.4570457994644658,
    1.445305721320277,
    -0.5900435899266435,
]


def sh_basis(dir_x, dir_y, dir_z):
    sq_x = dir_x * dir_x
    sq_y = dir_y * dir_y
    sq_z = dir_z * dir_z
    return [
        sh_zero + 0.0 * dir_x,
        -sh_one * dir_y,
        sh_one * dir_z,
        -sh_one * dir_x,
        sh_two[0] * dir_x * dir_y,
        sh_two[1] * dir_y * dir_z,
        sh_two[2] * (2.0 * sq_z - sq_x - sq_y),
        sh_two[3] * dir_x * dir_z,
        sh_two[4] * (sq_x - sq_y),
        sh_three[0] * dir_y * (3.0 * sq_x - sq_y),
        sh_three[1] * dir_x * dir_y * dir_z,
        sh_three[2] * dir_y * (4.0 * sq_z - sq_x - sq_y),
        sh_three[3] * dir_z * (2.0 * sq_z - 3.0 * sq_x - 3.0 * sq_y),
        sh_three[4] * dir_x * (4.0 * sq_z - sq_x - sq_y),
        sh_three[5] * dir_z * (sq_x - sq_y),
        sh_three[6] * dir_x * (sq_x - 3.0 * sq_y),
    ]


def screen(params, focal_len, centre_x, centre_y):
    mean_x, mean_y, depths = (params[0], params[1], params[2])
    scales = jnp.exp(params[3:6])
    quat = params[6:10]
    quat = quat / jnp.sqrt(jnp.sum(quat * quat, axis=0))
    quat_r, quat_i, quat_j, quat_k = (quat[0], quat[1], quat[2], quat[3])
    rotation = [
        [
            1.0 - 2.0 * (quat_j * quat_j + quat_k * quat_k),
            2.0 * (quat_i * quat_j - quat_r * quat_k),
            2.0 * (quat_i * quat_k + quat_r * quat_j),
        ],
        [
            2.0 * (quat_i * quat_j + quat_r * quat_k),
            1.0 - 2.0 * (quat_i * quat_i + quat_k * quat_k),
            2.0 * (quat_j * quat_k - quat_r * quat_i),
        ],
        [
            2.0 * (quat_i * quat_k - quat_r * quat_j),
            2.0 * (quat_j * quat_k + quat_r * quat_i),
            1.0 - 2.0 * (quat_i * quat_i + quat_j * quat_j),
        ],
    ]
    inv_z = 1.0 / depths
    diag_jac = focal_len * inv_z
    side_x = -focal_len * mean_x * inv_z * inv_z
    side_y = -focal_len * mean_y * inv_z * inv_z
    upper = [
        (diag_jac * rotation[0][column] + side_x * rotation[2][column]) * scales[column]
        for column in range(3)
    ]
    lower = [
        (diag_jac * rotation[1][column] + side_y * rotation[2][column]) * scales[column]
        for column in range(3)
    ]
    cov_xx = upper[0] * upper[0] + upper[1] * upper[1] + upper[2] * upper[2] + 0.3
    cov_xy = upper[0] * lower[0] + upper[1] * lower[1] + upper[2] * lower[2]
    cov_yy = lower[0] * lower[0] + lower[1] * lower[1] + lower[2] * lower[2] + 0.3
    determ = cov_xx * cov_yy - cov_xy * cov_xy
    screen_u = focal_len * mean_x * inv_z + centre_x
    screen_v = focal_len * mean_y * inv_z + centre_y
    opacity = jax.nn.sigmoid(params[10])
    distance = jnp.sqrt(mean_x * mean_x + mean_y * mean_y + depths * depths)
    basis = sh_basis(mean_x / distance, mean_y / distance, depths / distance)
    colors = [
        0.5
        + sum((basis[harmonic] * params[11 + 16 * channel + harmonic] for harmonic in range(16)))
        for channel in range(3)
    ]
    features = jnp.stack(
        [screen_u, screen_v, cov_yy / determ, -cov_xy / determ, cov_xx / determ, opacity] + colors,
        axis=0,
    )
    return features.reshape(9, -1, BLOCK).transpose(1, 0, 2)


def coords_of(tile_id, positions):
    pix_x = (tile_id % TILES_X * TILE_SIDE + positions % TILE_SIDE).astype(jnp.float32) + 0.5
    pix_y = (tile_id // TILES_X * TILE_SIDE + positions // TILE_SIDE).astype(jnp.float32) + 0.5
    return (pix_x, pix_y)


def pixel_coords(tile_id):
    return coords_of(tile_id, jnp.arange(TILE_SIDE * TILE_SIDE, dtype=jnp.int32))


def pair_terms(feature, pix_x, pix_y):
    off_x = pix_x[:, None] - feature[0][None, :]
    off_y = pix_y[:, None] - feature[1][None, :]
    exponent = (
        -0.5 * (feature[2][None, :] * off_x * off_x + feature[4][None, :] * off_y * off_y)
        - feature[3][None, :] * off_x * off_y
    )
    falloff = jnp.exp(exponent)
    return (off_x, off_y, falloff, feature[5][None, :] * falloff)


def tile_gradients(listed, live_count, cotangent, pix_x, pix_y):
    precise = lax.Precision.HIGHEST
    pixels = pix_x.shape[0]

    def forward(slot_idx, state_in):
        log_trans, colors = state_in
        feature = listed[slot_idx]
        alphas = pair_terms(feature, pix_x, pix_y)[3]
        log_keep = jnp.log(1.0 - alphas)
        before = jnp.cumsum(log_keep, axis=1) - log_keep
        weight = jnp.exp(log_trans[:, None] + before) * alphas
        colors = colors + jnp.dot(weight, feature[6:9].T, precision=precise)
        return (log_trans + jnp.sum(log_keep, axis=1), colors)

    start_state = (jnp.zeros((pixels,), jnp.float32), jnp.zeros((pixels, 3), jnp.float32))
    image = lax.fori_loop(0, live_count, forward, start_state)[1]

    def backward(slot_idx, state_in):
        log_trans, done, gradients = state_in
        feature = listed[slot_idx]
        off_x, off_y, falloff, alphas = pair_terms(feature, pix_x, pix_y)
        log_keep = jnp.log(1.0 - alphas)
        before = jnp.cumsum(log_keep, axis=1) - log_keep
        transmit = jnp.exp(log_trans[:, None] + before)
        weight = transmit * alphas
        dalpha = jnp.zeros_like(alphas)
        for channel in range(3):
            shaded = weight * feature[6 + channel][None, :]
            behind = (image[:, channel] - done[:, channel])[:, None] - jnp.cumsum(shaded, axis=1)
            dalpha = dalpha + cotangent[channel][:, None] * (
                transmit * feature[6 + channel][None, :] - behind / (1.0 - alphas)
            )
        dcolor = jnp.dot(cotangent, weight, precision=precise)
        dpower = dalpha * alphas
        sums_list = [
            jnp.sum(dpower * (feature[2][None, :] * off_x + feature[3][None, :] * off_y), axis=0),
            jnp.sum(dpower * (feature[3][None, :] * off_x + feature[4][None, :] * off_y), axis=0),
            -0.5 * jnp.sum(dpower * off_x * off_x, axis=0),
            -jnp.sum(dpower * off_x * off_y, axis=0),
            -0.5 * jnp.sum(dpower * off_y * off_y, axis=0),
            jnp.sum(dalpha * falloff, axis=0),
        ]
        block_grad = jnp.concatenate([jnp.stack(sums_list, axis=0), dcolor], axis=0)
        gradients = lax.dynamic_update_index_in_dim(gradients, block_grad, slot_idx, 0)
        done = done + jnp.dot(weight, feature[6:9].T, precision=precise)
        return (log_trans + jnp.sum(log_keep, axis=1), done, gradients)

    return lax.fori_loop(
        0, live_count, backward, (start_state[0], start_state[1], jnp.zeros_like(listed))
    )[2]


def body(params, blocks, counts, pixel_grad):
    tiles_dev = counts.shape[0]
    devices = lax.axis_size("dev")
    image_width = TILES_X * TILE_SIDE
    height = devices * tiles_dev // TILES_X * TILE_SIDE
    local_feat, pullback = jax.vjp(
        lambda values: screen(values, float(image_width), image_width / 2.0, height / 2.0), params
    )
    flat_ids = blocks.reshape(-1)
    pixels = TILE_SIDE * TILE_SIDE
    cotangent = pixel_grad.reshape(3, tiles_dev, pixels).transpose(1, 0, 2)
    first_tile = lax.axis_index("dev") * tiles_dev
    all_feat = lax.all_gather(local_feat, "dev", axis=0, tiled=True)

    def one_tile(tile_args):
        tile_num, tile_feat, live_count, tile_cot = tile_args
        pix_x, pix_y = pixel_coords(first_tile + tile_num)
        return tile_gradients(tile_feat, live_count, tile_cot, pix_x, pix_y)

    gradients = lax.map(
        one_tile, (jnp.arange(tiles_dev, dtype=jnp.int32), all_feat[blocks], counts, cotangent)
    )
    dense_grad = jnp.zeros_like(all_feat).at[flat_ids].add(gradients.reshape(-1, 9, BLOCK))
    feature_grad = lax.psum_scatter(dense_grad, "dev", scatter_dimension=0, tiled=True)
    return pullback(feature_grad)[0]


def solution(mesh):
    return jax.shard_map(
        body,
        mesh=mesh,
        in_specs=(P(None, "dev"), P("dev", None), P("dev"), P(None, "dev")),
        out_specs=P(None, "dev"),
        check_vma=False,
    )
```

profile of v0, /device:TPU:0, one launch (start us, length us, event | category | flops | bytes accessed | tf_op | source)
XLA Modules:
  0.0 2045.2 jit_solution(7160727513263844686)
XLA Ops:
  8.3 1.9 add_add_fusion.15
  10.2 1.9 add_add_fusion.16
  12.1 1.8 add_add_fusion.17
  14.9 1.8 fusion.145
  20.1 76.5 %all-gather.2.cloned.1.call-done = f32[2048,9,128]{2,0,1:T(8,128)} async-done(((f32[16,9,128]{2,0,1:T(8,128)}), f32[2048,9,128]{2,0,1:T(8,128)}) %all-gather.2.cloned.1.call-update) | async-done | bytes 9437200 | tf_op jit(solution)/shard_map/all_gather | solution.py:194
  96.6 12.8 copy.7
  109.4 7.4 gather_fusion
  117.3 464.8 %while.67 = (s32[]{:T(128)}, f32[4,32,9,128]{3,2,1,0:T(8,128)}, s32[4]{0:T(128)}, f32[4,32,9,128]{3,2,1,0:T(8,128)}, s32[4]{0:T(128)}, /*index=5*/s32[]{:T(128)}...) while((s32[]{:T(128)}, f32[4,32,9,128]{3,2,1,0:T(8,128)}, ...), condition=%wide.region_19.20_spmd, body=%wide.region_1.19_spmd.sunk | while | flops 113947312 | bytes 16455790 | solution.py:201
  117.3 1.2 dynamic_slice.47
  118.5 1.3 dynamic_slice.48
  122.3 24.7 %while.68 = (s32[]{:T(128)}, f32[1024]{0:T(1024)S(1)}, f32[1024,3]{0,1:T(4,128)S(1)}, s32[]{:T(128)}, f32[32,9,128]{2,1,0:T(8,128)S(1)}, /*index=5*/s32[]{:T(128...) while((s32[]{:T(128)}, f32[1024]{0:T(1024)S(1)}, ...), condition=%wide.region_5.5_spmd.clone, body=%wide.region_2.4_spmd.clone.sunk | while | flops 25318408 | bytes 2185531 | solution.py:145
  147.0 69.4 %while.69 = (s32[]{:T(128)}, f32[1024]{0:T(1024)S(1)}, f32[1024,3]{0,1:T(4,128)S(1)}, f32[32,9,128]{2,1,0:T(8,128)S(1)}, s32[]{:T(128)}, /*index=5*/f32[32,9,128...) while((s32[]{:T(128)}, f32[1024]{0:T(1024)S(1)}, ...), condition=%wide.region_18.18_spmd.clone, body=%wide.region_6.17_spmd.clone.sunk | while | flops 88628880 | bytes 13360023 | solution.py:177
  217.2 1.2 dynamic_slice.47
  218.4 1.3 dynamic_slice.48
  222.2 29.5 %while.68 = (s32[]{:T(128)}, f32[1024]{0:T(1024)S(1)}, f32[1024,3]{0,1:T(4,128)S(1)}, s32[]{:T(128)}, f32[32,9,128]{2,1,0:T(8,128)S(1)}, /*index=5*/s32[]{:T(128...) while((s32[]{:T(128)}, f32[1024]{0:T(1024)S(1)}, ...), condition=%wide.region_5.5_spmd.clone, body=%wide.region_2.4_spmd.clone.sunk | while | flops 25318408 | bytes 2185531 | solution.py:145
  251.7 83.2 %while.69 = (s32[]{:T(128)}, f32[1024]{0:T(1024)S(1)}, f32[1024,3]{0,1:T(4,128)S(1)}, f32[32,9,128]{2,1,0:T(8,128)S(1)}, s32[]{:T(128)}, /*index=5*/f32[32,9,128...) while((s32[]{:T(128)}, f32[1024]{0:T(1024)S(1)}, ...), condition=%wide.region_18.18_spmd.clone, body=%wide.region_6.17_spmd.clone.sunk | while | flops 88628880 | bytes 13360023 | solution.py:177
  335.7 1.2 dynamic_slice.47
  336.9 1.3 dynamic_slice.48
  340.7 24.7 %while.68 = (s32[]{:T(128)}, f32[1024]{0:T(1024)S(1)}, f32[1024,3]{0,1:T(4,128)S(1)}, s32[]{:T(128)}, f32[32,9,128]{2,1,0:T(8,128)S(1)}, /*index=5*/s32[]{:T(128...) while((s32[]{:T(128)}, f32[1024]{0:T(1024)S(1)}, ...), condition=%wide.region_5.5_spmd.clone, body=%wide.region_2.4_spmd.clone.sunk | while | flops 25318408 | bytes 2185531 | solution.py:145
  365.4 69.4 %while.69 = (s32[]{:T(128)}, f32[1024]{0:T(1024)S(1)}, f32[1024,3]{0,1:T(4,128)S(1)}, f32[32,9,128]{2,1,0:T(8,128)S(1)}, s32[]{:T(128)}, /*index=5*/f32[32,9,128...) while((s32[]{:T(128)}, f32[1024]{0:T(1024)S(1)}, ...), condition=%wide.region_18.18_spmd.clone, body=%wide.region_6.17_spmd.clone.sunk | while | flops 88628880 | bytes 13360023 | solution.py:177
  435.6 1.2 dynamic_slice.47
  436.9 1.3 dynamic_slice.48
  440.6 36.7 %while.68 = (s32[]{:T(128)}, f32[1024]{0:T(1024)S(1)}, f32[1024,3]{0,1:T(4,128)S(1)}, s32[]{:T(128)}, f32[32,9,128]{2,1,0:T(8,128)S(1)}, /*index=5*/s32[]{:T(128...) while((s32[]{:T(128)}, f32[1024]{0:T(1024)S(1)}, ...), condition=%wide.region_5.5_spmd.clone, body=%wide.region_2.4_spmd.clone.sunk | while | flops 25318408 | bytes 2185531 | solution.py:145
  477.4 103.9 %while.69 = (s32[]{:T(128)}, f32[1024]{0:T(1024)S(1)}, f32[1024,3]{0,1:T(4,128)S(1)}, f32[32,9,128]{2,1,0:T(8,128)S(1)}, s32[]{:T(128)}, /*index=5*/f32[32,9,128...) while((s32[]{:T(128)}, f32[1024]{0:T(1024)S(1)}, ...), condition=%wide.region_18.18_spmd.clone, body=%wide.region_6.17_spmd.clone.sunk | while | flops 88628880 | bytes 13360023 | solution.py:177
  502.8 1.0 multiply_multiply_fusion.30
  582.1 6.0 broadcast_in_dim.29
  588.1 14.4 scatter_fusion
  602.6 1423.9 %reduce-scatter.2.cloned.1.call-done = f32[16,9,128]{2,1,0:T(8,128)} async-done(((f32[2048,9,128]{2,1,0:T(8,128)}), f32[16,9,128]{2,1,0:T(8,128)}) %reduce-scatter.2.cloned.1.call-update) | async-done | bytes 73744 | tf_op jit(solution)/shard_map/reduce_scatter | solution.py:205
  2026.5 1.1 fusion.118
  2031.3 1.9 fusion.80
  2034.2 1.1 fusion.100
  2036.4 2.0 pad_add_fusion
  (1365 shorter events, 397.3 us)
Async XLA Ops:
  6.5 90.1 %all-gather.2.cloned.1.call-start = ((), (), s32[]{:S(2)}) async-start(), calls=%async_computation.1 | async-start | bytes 9510912 | tf_op jit(solution)/shard_map/all_gather | solution.py:194
  17.8 0.6 copy-start.2
  18.4 2008.0 %reduce-scatter.2.cloned.1.call-start = ((), (), s32[]{:S(2)}) async-start(), calls=%async_computation.2 | async-start | bytes 16908288 | tf_op jit(solution)/shard_map/reduce_scatter | solution.py:205
  582.0 6.1 copy-start.1
  582.0 1446.6 %copy-start.10 = (f32[1,2048]{1,0:T(1,128)S(1)}, f32[1,2048]{1,0:T(1,128)}, u32[]{:S(2)}) copy-start(f32[1,2048]{1,0:T(1,128)} %get-tuple-element.361) | copy-start | bytes 24580
  582.0 1448.5 %copy-start.4 = (f32[1,2048]{1,0:T(1,128)S(1)}, f32[1,2048]{1,0:T(1,128)}, u32[]{:S(2)}) copy-start(f32[1,2048]{1,0:T(1,128)} %get-tuple-element.363) | copy-start | bytes 24580
  582.0 1448.6 %copy-start.5 = (f32[1,2048]{1,0:T(1,128)S(1)}, f32[1,2048]{1,0:T(1,128)}, u32[]{:S(2)}) copy-start(f32[1,2048]{1,0:T(1,128)} %get-tuple-element.365) | copy-start | bytes 24580
  582.0 1448.6 %copy-start.6 = (f32[1,2048]{1,0:T(1,128)S(1)}, f32[1,2048]{1,0:T(1,128)}, u32[]{:S(2)}) copy-start(f32[1,2048]{1,0:T(1,128)} %get-tuple-element.367) | copy-start | bytes 24580
  582.0 1448.6 %copy-start.7 = (f32[1,2048]{1,0:T(1,128)S(1)}, f32[1,2048]{1,0:T(1,128)}, u32[]{:S(2)}) copy-start(f32[1,2048]{1,0:T(1,128)} %get-tuple-element.371) | copy-start | bytes 24580
  582.1 1448.6 %copy-start.8 = (f32[1,2048]{1,0:T(1,128)S(1)}, f32[1,2048]{1,0:T(1,128)}, u32[]{:S(2)}) copy-start(f32[1,2048]{1,0:T(1,128)} %get-tuple-element.374) | copy-start | bytes 24580
  582.1 1448.6 %copy-start.9 = (f32[1,2048]{1,0:T(1,128)S(1)}, f32[1,2048]{1,0:T(1,128)}, u32[]{:S(2)}) copy-start(f32[1,2048]{1,0:T(1,128)} %get-tuple-element.377) | copy-start | bytes 24580
  582.1 1449.0 %copy-start = (f32[59,2048]{1,0:T(8,128)S(1)}, f32[59,2048]{1,0:T(8,128)}, u32[]{:S(2)}) copy-start(f32[59,2048]{1,0:T(8,128)} %param.10) | copy-start | bytes 1449988
  582.1 1449.1 %copy-start.3 = (f32[1,2048]{1,0:T(1,128)S(1)}, f32[1,2048]{1,0:T(1,128)}, u32[]{:S(2)}) copy-start(f32[1,2048]{1,0:T(1,128)} %get-tuple-element.364) | copy-start | bytes 24580
Sparse Core Ops, SparseCore 0:
  18.6 77.9 all-gather.1
  602.7 1423.7 reduce-scatter.1
where the time goes:
time: 2050 us
  waiting for transfers between devices  1500 us (73%)
  other arithmetic  321 us (16%)
  matrix products  83.6 us (4%)
  loops' own time  68.4 us (3%)
  local copies, waits for them, and re-layouts  58 us (3%)
    reduce_scatter x1, waiting for transfers between devices, body(): lax.psum_scatter(dense_grad, 'dev', scatter_dimension=0, tiled=True)  1420 us
    all_gather x1, waiting for transfers between devices, body(): all_feat = lax.all_gather(local_feat, 'dev', axis=0, tiled=True)  76.5 us
    another operation x141, other arithmetic, backward(): jnp.cumsum(shaded, axis=1)  68.6 us
    mul x47, other arithmetic, backward(): dpower = dalpha * alphas  48.8 us
    reduce_sum x47, other arithmetic, backward(): jnp.sum(dpower * (feature[3][None, :] * off_x + feature[4][None, :] * off...  44 us
  transfers between devices with their start and end apart: 2, of which 2 were waited for; matrix products, arithmetic and copies ran while one was open for 0% of the time, Pallas kernels for 0%

commit v1 on v0

--- a/solution.py
+++ b/solution.py
@@ -191,7 +191,9 @@
     pixels = TILE_SIDE * TILE_SIDE
     cotangent = pixel_grad.reshape(3, tiles_dev, pixels).transpose(1, 0, 2)
     first_tile = lax.axis_index("dev") * tiles_dev
-    all_feat = lax.all_gather(local_feat, "dev", axis=0, tiled=True)
+    all_feat = jnp.concatenate(
+        lax.all_to_all(jnp.stack([local_feat] * lax.axis_size("dev")), "dev", 0, 0), axis=0
+    )
 
     def one_tile(tile_args):
         tile_num, tile_feat, live_count, tile_cot = tile_args

time: 2050 us -> 2120 us (1.034)
  waiting for transfers between devices: 1500 us -> 1540 us
    all_to_all x0 -> x1, waiting for transfers between devices: none -> 115 us  [body(): lax.all_to_all(jnp.stack([local_feat] * lax.axis_size('dev')), 'dev', 0, 0)]
    all_gather x1 -> x0, waiting for transfers between devices: 76.5 us -> none  [body(): all_feat = lax.all_gather(local_feat, 'dev', axis=0, tiled=True)]
    reshape x0 -> x1, local copies, waits for them, and re-layouts: none -> 22.5 us  [body(): jnp.concatenate(lax.all_to_all(jnp.stack([local_feat] * lax.axis_size('de...]
where the time goes in v1:
time: 2120 us
  waiting for transfers between devices  1540 us (73%)
  other arithmetic  321 us (15%)
  matrix products  83.6 us (4%)
  loops' own time  72.5 us (3%)
  local copies, waits for them, and re-layouts  69.9 us (3%)
    reduce_scatter x1, waiting for transfers between devices, body(): lax.psum_scatter(dense_grad, 'dev', scatter_dimension=0, tiled=True)  1430 us
    all_to_all x1, waiting for transfers between devices, body(): lax.all_to_all(jnp.stack([local_feat] * lax.axis_size('dev')), 'dev', 0, 0)  115 us
    another operation x141, other arithmetic, backward(): jnp.cumsum(shaded, axis=1)  68.6 us
    mul x47, other arithmetic, backward(): dpower = dalpha * alphas  48.8 us
    reduce_sum x47, other arithmetic, backward(): jnp.sum(dpower * (feature[3][None, :] * off_x + feature[4][None, :] * off...  44 us
  transfers between devices with their start and end apart: 2, of which 2 were waited for; matrix products, arithmetic and copies ran while one was open for 0% of the time, Pallas kernels for 0%

profile of v1, /device:TPU:0, one launch (start us, length us, event | category | flops | bytes accessed | tf_op | source)
XLA Modules:
  0.0 2116.9 jit_solution(13888098301883710079)
XLA Ops:
  8.4 2.5 add_add_fusion.15
  10.9 1.7 add_add_fusion.16
  12.6 1.8 add_add_fusion.17
  16.6 1.9 fusion.145
  19.6 4.2 stack.38
  23.9 11.6 all-to-all-start
  35.8 114.9 %all-to-all-done = f32[128,16,9,128]{3,1,2,0:T(8,128)} async-done(((f32[128,16,9,128]{3,1,2,0:T(8,128)}), f32[128,16,9,128]{3,1,2,0:T(8,128)}, u32[]{:S(2)}, u32[]{:S(2)}) %all-to-all-start) | async-done | bytes 9437216 | tf_op jit(solution)/shard_map/all_to_all | solution.py:195
  150.7 4.6 copy.10
  155.3 22.5 %copy.11 = f32[2048,9,128]{2,1,0:T(8,128)} copy(f32[2048,9,128]{2,0,1:T(8,128)S(1)} %bitcast.306) | data formatting | bytes 18874368 | tf_op jit(solution)/shard_map/reshape | solution.py:194
  177.8 7.4 gather_fusion
  185.2 463.2 %while.67 = (s32[]{:T(128)}, f32[4,32,9,128]{3,2,1,0:T(8,128)}, s32[4]{0:T(128)S(1)}, f32[4,32,9,128]{3,2,1,0:T(8,128)}, s32[4]{0:T(128)S(1)}, /*index=5*/s32[]{...) while((s32[]{:T(128)}, f32[4,32,9,128]{3,2,1,0:T(8,128)}, ...), condition=%wide.region_19.20_spmd, body=%wide.region_1.19_spmd.sunk | while | flops 113947312 | bytes 16455790 | solution.py:203
  188.7 25.2 %while.68 = (s32[]{:T(128)}, f32[1024]{0:T(1024)S(1)}, f32[1024,3]{0,1:T(4,128)S(1)}, s32[]{:T(128)}, f32[32,9,128]{2,1,0:T(8,128)S(1)}, /*index=5*/s32[]{:T(128...) while((s32[]{:T(128)}, f32[1024]{0:T(1024)S(1)}, ...), condition=%wide.region_5.5_spmd.clone, body=%wide.region_2.4_spmd.clone.sunk | while | flops 25318408 | bytes 2185531 | solution.py:145
  213.9 69.9 %while.69 = (s32[]{:T(128)}, f32[1024]{0:T(1024)S(1)}, f32[1024,3]{0,1:T(4,128)S(1)}, f32[32,9,128]{2,1,0:T(8,128)S(1)}, s32[]{:T(128)}, /*index=5*/f32[32,9,128...) while((s32[]{:T(128)}, f32[1024]{0:T(1024)S(1)}, ...), condition=%wide.region_18.18_spmd.clone, body=%wide.region_6.17_spmd.clone.sunk | while | flops 88628880 | bytes 13360023 | solution.py:177
  218.7 1.0 multiply_multiply_fusion.30
  225.6 1.0 multiply_multiply_fusion.30
  288.1 30.1 %while.68 = (s32[]{:T(128)}, f32[1024]{0:T(1024)S(1)}, f32[1024,3]{0,1:T(4,128)S(1)}, s32[]{:T(128)}, f32[32,9,128]{2,1,0:T(8,128)S(1)}, /*index=5*/s32[]{:T(128...) while((s32[]{:T(128)}, f32[1024]{0:T(1024)S(1)}, ...), condition=%wide.region_5.5_spmd.clone, body=%wide.region_2.4_spmd.clone.sunk | while | flops 25318408 | bytes 2185531 | solution.py:145
  318.2 83.8 %while.69 = (s32[]{:T(128)}, f32[1024]{0:T(1024)S(1)}, f32[1024,3]{0,1:T(4,128)S(1)}, f32[32,9,128]{2,1,0:T(8,128)S(1)}, s32[]{:T(128)}, /*index=5*/f32[32,9,128...) while((s32[]{:T(128)}, f32[1024]{0:T(1024)S(1)}, ...), condition=%wide.region_18.18_spmd.clone, body=%wide.region_6.17_spmd.clone.sunk | while | flops 88628880 | bytes 13360023 | solution.py:177
  406.2 25.2 %while.68 = (s32[]{:T(128)}, f32[1024]{0:T(1024)S(1)}, f32[1024,3]{0,1:T(4,128)S(1)}, s32[]{:T(128)}, f32[32,9,128]{2,1,0:T(8,128)S(1)}, /*index=5*/s32[]{:T(128...) while((s32[]{:T(128)}, f32[1024]{0:T(1024)S(1)}, ...), condition=%wide.region_5.5_spmd.clone, body=%wide.region_2.4_spmd.clone.sunk | while | flops 25318408 | bytes 2185531 | solution.py:145
  431.5 69.9 %while.69 = (s32[]{:T(128)}, f32[1024]{0:T(1024)S(1)}, f32[1024,3]{0,1:T(4,128)S(1)}, f32[32,9,128]{2,1,0:T(8,128)S(1)}, s32[]{:T(128)}, /*index=5*/f32[32,9,128...) while((s32[]{:T(128)}, f32[1024]{0:T(1024)S(1)}, ...), condition=%wide.region_18.18_spmd.clone, body=%wide.region_6.17_spmd.clone.sunk | while | flops 88628880 | bytes 13360023 | solution.py:177
  498.6 1.0 multiply_multiply_fusion.30
  505.6 37.5 %while.68 = (s32[]{:T(128)}, f32[1024]{0:T(1024)S(1)}, f32[1024,3]{0,1:T(4,128)S(1)}, s32[]{:T(128)}, f32[32,9,128]{2,1,0:T(8,128)S(1)}, /*index=5*/s32[]{:T(128...) while((s32[]{:T(128)}, f32[1024]{0:T(1024)S(1)}, ...), condition=%wide.region_5.5_spmd.clone, body=%wide.region_2.4_spmd.clone.sunk | while | flops 25318408 | bytes 2185531 | solution.py:145
  543.1 104.6 %while.69 = (s32[]{:T(128)}, f32[1024]{0:T(1024)S(1)}, f32[1024,3]{0,1:T(4,128)S(1)}, f32[32,9,128]{2,1,0:T(8,128)S(1)}, s32[]{:T(128)}, /*index=5*/f32[32,9,128...) while((s32[]{:T(128)}, f32[1024]{0:T(1024)S(1)}, ...), condition=%wide.region_18.18_spmd.clone, body=%wide.region_6.17_spmd.clone.sunk | while | flops 88628880 | bytes 13360023 | solution.py:177
  575.6 1.0 multiply_multiply_fusion.30
  582.5 1.0 multiply_multiply_fusion.30
  631.1 1.0 multiply_multiply_fusion.30
  648.8 6.0 broadcast_in_dim.29
  654.8 14.5 scatter_fusion
  669.3 1428.7 %reduce-scatter.2.cloned.1.call-done = f32[16,9,128]{2,1,0:T(8,128)} async-done(((f32[2048,9,128]{2,1,0:T(8,128)}), f32[16,9,128]{2,1,0:T(8,128)}) %reduce-scatter.2.cloned.1.call-update) | async-done | bytes 73744 | tf_op jit(solution)/shard_map/reduce_scatter | solution.py:207
  2098.0 1.1 fusion.118
  2103.0 1.9 fusion.80
  2105.9 1.1 fusion.100
  2108.1 2.0 pad_add_fusion
  (1458 shorter events, 395.5 us)
Async XLA Ops:
  23.9 126.8 %all-to-all-start = ((f32[128,16,9,128]{3,1,2,0:T(8,128)}), f32[128,16,9,128]{3,1,2,0:T(8,128)}, u32[]{:S(2)}, u32[]{:S(2)}) async-start(f32[128,16,9,128]{3,1,2,0:T(8,128)} %stack.38), calls=%async_computation | async-start | bytes 18874368 | tf_op jit(solution)/shard_map/all_to_all | solution.py:195
  35.5 2062.5 %reduce-scatter.2.cloned.1.call-start = ((), (), s32[]{:S(2)}) async-start(), calls=%async_computation.2 | async-start | bytes 16908288 | tf_op jit(solution)/shard_map/reduce_scatter | solution.py:207
  648.5 1451.7 %copy-start.20 = (f32[1,2048]{1,0:T(1,128)S(1)}, f32[1,2048]{1,0:T(1,128)}, u32[]{:S(2)}) copy-start(f32[1,2048]{1,0:T(1,128)} %copy-done.19) | copy-start | bytes 24580
  648.5 1451.7 %copy-start.22 = (f32[1,2048]{1,0:T(1,128)S(1)}, f32[1,2048]{1,0:T(1,128)}, u32[]{:S(2)}) copy-start(f32[1,2048]{1,0:T(1,128)} %copy-done.21) | copy-start | bytes 24580
  648.5 1451.7 %copy-start.24 = (f32[1,2048]{1,0:T(1,128)S(1)}, f32[1,2048]{1,0:T(1,128)}, u32[]{:S(2)}) copy-start(f32[1,2048]{1,0:T(1,128)} %copy-done.23) | copy-start | bytes 24580
  648.5 1453.6 %copy-start.2 = (f32[4,2048]{1,0:T(4,128)S(1)}, f32[4,2048]{1,0:T(4,128)}, u32[]{:S(2)}) copy-start(f32[4,2048]{1,0:T(4,128)} %copy-done.1) | copy-start | bytes 98308
  648.5 1453.6 %copy-start.5 = (f32[1,2048]{1,0:T(1,128)S(1)}, f32[1,2048]{1,0:T(1,128)}, u32[]{:S(2)}) copy-start(f32[1,2048]{1,0:T(1,128)} %copy-done.4) | copy-start | bytes 24580
  648.5 1453.6 %copy-start.15 = (f32[3,2048]{1,0:T(4,128)S(1)}, f32[3,2048]{1,0:T(4,128)}, u32[]{:S(2)}) copy-start(f32[3,2048]{1,0:T(4,128)} %copy-done.14) | copy-start | bytes 73732
  648.5 1453.6 %copy-start.37 = (f32[1,2048]{1,0:T(1,128)S(1)}, f32[1,2048]{1,0:T(1,128)}, u32[]{:S(2)}) copy-start(f32[1,2048]{1,0:T(1,128)} %get-tuple-element.376) | copy-start | bytes 24580
  648.6 1453.6 %copy-start.38 = (f32[1,2048]{1,0:T(1,128)S(1)}, f32[1,2048]{1,0:T(1,128)}, u32[]{:S(2)}) copy-start(f32[1,2048]{1,0:T(1,128)} %get-tuple-element.386) | copy-start | bytes 24580
  648.6 1453.6 %copy-start.48 = (f32[1,2048]{1,0:T(1,128)S(1)}, f32[1,2048]{1,0:T(1,128)}, u32[]{:S(2)}) copy-start(f32[1,2048]{1,0:T(1,128)} %get-tuple-element.370) | copy-start | bytes 24580
  648.6 1453.6 %copy-start.49 = (f32[1,2048]{1,0:T(1,128)S(1)}, f32[1,2048]{1,0:T(1,128)}, u32[]{:S(2)}) copy-start(f32[1,2048]{1,0:T(1,128)} %get-tuple-element.372) | copy-start | bytes 24580
  648.6 1453.6 %copy-start.50 = (f32[1,2048]{1,0:T(1,128)S(1)}, f32[1,2048]{1,0:T(1,128)}, u32[]{:S(2)}) copy-start(f32[1,2048]{1,0:T(1,128)} %get-tuple-element.374) | copy-start | bytes 24580
  648.6 1453.6 %copy-start.51 = (f32[1,2048]{1,0:T(1,128)S(1)}, f32[1,2048]{1,0:T(1,128)}, u32[]{:S(2)}) copy-start(f32[1,2048]{1,0:T(1,128)} %get-tuple-element.378) | copy-start | bytes 24580
  648.6 1453.6 %copy-start.52 = (f32[1,2048]{1,0:T(1,128)S(1)}, f32[1,2048]{1,0:T(1,128)}, u32[]{:S(2)}) copy-start(f32[1,2048]{1,0:T(1,128)} %get-tuple-element.381) | copy-start | bytes 24580
  648.6 1453.6 %copy-start.53 = (f32[1,2048]{1,0:T(1,128)S(1)}, f32[1,2048]{1,0:T(1,128)}, u32[]{:S(2)}) copy-start(f32[1,2048]{1,0:T(1,128)} %get-tuple-element.384) | copy-start | bytes 24580
  648.6 1454.0 %copy-start = (f32[59,2048]{1,0:T(8,128)S(1)}, f32[59,2048]{1,0:T(8,128)}, u32[]{:S(2)}) copy-start(f32[59,2048]{1,0:T(8,128)} %param.10) | copy-start | bytes 1449988
  648.6 1454.0 %copy-start.44 = (f32[2048]{0:T(1024)S(1)}, f32[2048]{0:T(1024)}, u32[]{:S(2)}) copy-start(f32[2048]{0:T(1024)} %get-tuple-element.492) | copy-start | bytes 24580
  648.6 1454.1 %copy-start.36 = (f32[2048]{0:T(1024)S(1)}, f32[2048]{0:T(1024)}, u32[]{:S(2)}) copy-start(f32[2048]{0:T(1024)} %copy-done.35) | copy-start | bytes 24580
  648.7 1454.1 %copy-start.34 = (f32[2048]{0:T(1024)S(1)}, f32[2048]{0:T(1024)}, u32[]{:S(2)}) copy-start(f32[2048]{0:T(1024)} %copy-done.33) | copy-start | bytes 24580
  648.7 1454.2 %copy-start.47 = (f32[1,2048]{1,0:T(1,128)S(1)}, f32[1,2048]{1,0:T(1,128)}, u32[]{:S(2)}) copy-start(f32[1,2048]{1,0:T(1,128)} %get-tuple-element.371) | copy-start | bytes 24580
  648.7 1454.2 %copy-start.46 = (f32[1,2048]{1,0:T(1,128)S(1)}, f32[1,2048]{1,0:T(1,128)}, u32[]{:S(2)}) copy-start(f32[1,2048]{1,0:T(1,128)} %get-tuple-element.373) | copy-start | bytes 24580
  648.7 1454.2 %copy-start.45 = (f32[1,2048]{1,0:T(1,128)S(1)}, f32[1,2048]{1,0:T(1,128)}, u32[]{:S(2)}) copy-start(f32[1,2048]{1,0:T(1,128)} %get-tuple-element.375) | copy-start | bytes 24580
  648.7 1454.2 %copy-start.43 = (f32[1,2048]{1,0:T(1,128)S(1)}, f32[1,2048]{1,0:T(1,128)}, u32[]{:S(2)}) copy-start(f32[1,2048]{1,0:T(1,128)} %get-tuple-element.379) | copy-start | bytes 24580
  648.7 1454.2 %copy-start.42 = (f32[1,2048]{1,0:T(1,128)S(1)}, f32[1,2048]{1,0:T(1,128)}, u32[]{:S(2)}) copy-start(f32[1,2048]{1,0:T(1,128)} %get-tuple-element.385) | copy-start | bytes 24580
  648.7 1454.3 %copy-start.41 = (f32[1,2048]{1,0:T(1,128)S(1)}, f32[1,2048]{1,0:T(1,128)}, u32[]{:S(2)}) copy-start(f32[1,2048]{1,0:T(1,128)} %get-tuple-element.382) | copy-start | bytes 24580
  648.7 1454.3 %copy-start.16 = (f32[1,2048]{1,0:T(1,128)S(1)}, f32[1,2048]{1,0:T(1,128)}, u32[]{:S(2)}) copy-start(f32[1,2048]{1,0:T(1,128)} %get-tuple-element.380) | copy-start | bytes 24580
  648.7 1454.3 %copy-start.17 = (f32[1,2048]{1,0:T(1,128)S(1)}, f32[1,2048]{1,0:T(1,128)}, u32[]{:S(2)}) copy-start(f32[1,2048]{1,0:T(1,128)} %get-tuple-element.383) | copy-start | bytes 24580
  648.7 1454.3 %copy-start.18 = (f32[1,2048]{1,0:T(1,128)S(1)}, f32[1,2048]{1,0:T(1,128)}, u32[]{:S(2)}) copy-start(f32[1,2048]{1,0:T(1,128)} %get-tuple-element.365) | copy-start | bytes 24580
  648.8 1458.3 %copy-start.28 = (f32[1,2048]{1,0:T(1,128)S(1)}, f32[1,2048]{1,0:T(1,128)}, u32[]{:S(2)}) copy-start(f32[1,2048]{1,0:T(1,128)} %copy-done.27) | copy-start | bytes 24580
  648.8 1458.3 %copy-start.30 = (f32[1,2048]{1,0:T(1,128)S(1)}, f32[1,2048]{1,0:T(1,128)}, u32[]{:S(2)}) copy-start(f32[1,2048]{1,0:T(1,128)} %copy-done.29) | copy-start | bytes 24580
  648.8 1458.3 %copy-start.32 = (f32[1,2048]{1,0:T(1,128)S(1)}, f32[1,2048]{1,0:T(1,128)}, u32[]{:S(2)}) copy-start(f32[1,2048]{1,0:T(1,128)} %copy-done.31) | copy-start | bytes 24580
  (27 other events, 11094.9 us)
Sparse Core Ops, SparseCore 0:
  669.4 1428.5 reduce-scatter.1
